TPU v7x, 32 devices: a whole 2x2x4 slice. The times are simulated.
32 devices in a mesh: dp: 4 (over y, x), seq: 8 (over z, core).
Axes of the slice: x: 2, y: 2, z: 4, core: 2. Of those that a mesh axis runs over, the one named last changes fastest.
Arguments:
- tokens: bfloat16 [4, 1280, 2048], P('dp', 'seq'), may hold values from -6 to 6
- w_query: bfloat16 [2048, 2048], P(('dp', 'seq')), may hold values from -0.125 to 0.125
- w_key: bfloat16 [2048, 2048], P(('dp', 'seq')), may hold values from -0.125 to 0.125
- w_value: bfloat16 [2048, 2048], P(('dp', 'seq')), may hold values from -0.125 to 0.125
- w_out: bfloat16 [2048, 2048], P(None, ('dp', 'seq')), may hold values from -0.125 to 0.125
- w_gate: bfloat16 [2048, 8192], P(('dp', 'seq')), may hold values from -0.125 to 0.125
- w_up: bfloat16 [2048, 8192], P(('dp', 'seq')), may hold values from -0.125 to 0.125
- w_down: bfloat16 [8192, 2048], P(None, ('dp', 'seq')), may hold values from -0.0625 to 0.0625
- gain_query: bfloat16 [2048], P(('dp', 'seq')), may hold values from 0.5 to 1.5
- gain_key: bfloat16 [2048], P(('dp', 'seq')), may hold values from 0.5 to 1.5
- gain_attn: bfloat16 [2048], P(('dp', 'seq')), may hold values from 0.5 to 1.5
- gain_mlp: bfloat16 [2048], P(('dp', 'seq')), may hold values from 0.5 to 1.5
- cotangent: bfloat16 [4, 1280, 2048], P('dp', 'seq'), may hold values from -6 to 6
- key_mask: int32 [4, 1280], P('dp', 'seq'), may hold values 0 or 1
- lengths: int32 [4], P('dp'), may hold values from 640 to 1280, as said below
- tract_order: int32 [4, 16], P('dp', 'seq'), may hold values from 0 to 15, as said below
Outputs:
- layer_out: bfloat16 [4, 1280, 2048], P('dp', 'seq')
- grad_tokens: bfloat16 [4, 1280, 2048], P('dp', 'seq')
- grad_w_query: float32 [2048, 2048], P(('dp', 'seq'))
- grad_w_key: float32 [2048, 2048], P(('dp', 'seq'))
- grad_w_value: float32 [2048, 2048], P(('dp', 'seq'))
- grad_w_out: float32 [2048, 2048], P(None, ('dp', 'seq'))
- grad_w_gate: float32 [2048, 8192], P(('dp', 'seq'))
- grad_w_up: float32 [2048, 8192], P(('dp', 'seq'))
- grad_w_down: float32 [8192, 2048], P(None, ('dp', 'seq'))
- grad_gain_query: float32 [2048], P(('dp', 'seq'))
- grad_gain_key: float32 [2048], P(('dp', 'seq'))
- grad_gain_attn: float32 [2048], P(('dp', 'seq'))
- grad_gain_mlp: float32 [2048], P(('dp', 'seq'))
Inputs may be any that keep to these rules, and one draw needn't show every extreme that they name: `lengths`: some row has all 1280 tokens valid. `tract_order`: each row is a permutation of 0 to 15: entry j is the place, in units of 80 tokens, of the row's j-th stored block.
All inputs are finite; a program needn't handle non-finite values. No bound on the sum of `key_mask` on one device may be relied on, other than what follows from the above.
Results may differ from a plain program's by a relative error of at most 0.02.
Values may be sent and summed in bfloat16 or wider, within the bound.
A program may use at most 768 MiB of HBM per device.

v0:
```python
import jax
import jax.numpy as jnp
from jax import lax
from jax.sharding import PartitionSpec as P

HEAD_DIM = 128
rope_base = 500000.0
norm_eps = 1e-06
f32 = jnp.float32
bf16 = jnp.bfloat16


def rms_factor(values):
    return lax.rsqrt(jnp.mean(values * values, axis=-1, keepdims=True) + norm_eps)


def norm_back(grad_normed, raw_values, factor):
    unit_values = raw_values * factor
    return factor * (
        grad_normed - unit_values * jnp.mean(grad_normed * unit_values, axis=-1, keepdims=True)
    )


def rope_tables(positions, head_dim):
    half_dim = head_dim // 2
    steps_f = jnp.arange(half_dim).astype(f32) * (2.0 / head_dim)
    inv_freq = jnp.power(rope_base, -steps_f)
    angle = positions.astype(f32)[:, None] * inv_freq[None, :]
    angle = jnp.concatenate([angle, angle], axis=-1)[:, None, :]
    return (jnp.cos(angle), jnp.sin(angle))


def rotate(values, cosine, sine):
    half_dim = values.shape[-1] // 2
    turned = jnp.concatenate([-values[..., half_dim:], values[..., :half_dim]], axis=-1)
    return values * cosine + turned * sine


def unrotate(grads, cosine, sine):
    half_dim = grads.shape[-1] // 2
    moved = grads * sine
    back_part = jnp.concatenate([moved[..., half_dim:], -moved[..., :half_dim]], axis=-1)
    return grads * cosine + back_part


def allowed_mask(query_pos, key_code):
    key_pos = key_code // 2
    usable = key_code % 2 == 1
    causal = key_pos[None, :] <= query_pos[:, None]
    return causal & (usable[None, :] | (key_pos[None, :] == query_pos[:, None]))


def dot_nn(left, right):
    return jnp.dot(left, right, preferred_element_type=f32)


def dot_nt(left, right):
    return lax.dot_general(left, right, (((1,), (1,)), ((), ())), preferred_element_type=f32)


def dot_tn(left, right):
    return lax.dot_general(left, right, (((0,), (0,)), ((), ())), preferred_element_type=f32)


def spread_columns(parts, ways):
    rows = parts[0].shape[0]
    split = [p.reshape(rows, ways, p.shape[1] // ways) for p in parts]
    joined = jnp.concatenate(split, axis=2)
    return joined.reshape(rows, ways * joined.shape[2])


def collect(matrix):
    moved = lax.all_to_all(matrix, "seq", split_axis=1, concat_axis=0, tiled=True)
    return lax.all_gather(moved, "dp", axis=0, tiled=True)


def gather_rows(rows):
    return lax.all_gather(rows, "seq", axis=0, tiled=True)


def scatter_rows(partial_rows):
    return lax.psum_scatter(
        partial_rows.astype(bf16), "seq", scatter_dimension=0, tiled=True
    ).astype(f32)


def return_grads(grad, widths, ways):
    summed = lax.psum_scatter(grad.astype(bf16), "dp", scatter_dimension=0, tiled=True)
    rows = summed.shape[0] // ways
    moved = lax.all_to_all(summed, "seq", split_axis=0, concat_axis=1, tiled=True)
    moved = moved.reshape(rows, ways, sum(widths))
    outs, begin = ([], 0)
    for width in widths:
        outs.append(moved[:, :, begin : begin + width].reshape(rows, ways * width).astype(f32))
        begin += width
    return outs


def body(
    tokens,
    w_query,
    w_key,
    w_value,
    w_out,
    w_gate,
    w_up,
    w_down,
    gain_query,
    gain_key,
    gain_attn,
    gain_mlp,
    cotangent,
    key_mask,
    lengths,
    tract_order,
):
    ways = lax.axis_size("seq")
    me = lax.axis_index("seq")
    token_rows = tokens[0]
    tok_count, feat_width = token_rows.shape
    ff_width = w_gate.shape[1]
    own_feat = feat_width // ways
    own_heads = own_feat // HEAD_DIM
    own_ff = ff_width // ways
    row_len = tok_count * ways
    score_scale = HEAD_DIM ** (-0.5)
    half_len = tok_count // 2
    order_pair = tract_order[0]
    slot_index = jnp.arange(tok_count, dtype=jnp.int32)
    local_pos = (
        jnp.where(slot_index < half_len, order_pair[0], order_pair[1]) * half_len
        + slot_index % half_len
    )
    key_ok = ((key_mask[0] == 1) & (local_pos < lengths[0])).astype(jnp.int32)
    grad_out = cotangent[0].astype(f32)
    gain_local = jnp.stack([gain_query, gain_key, gain_attn, gain_mlp], axis=1)
    gain_pad = jnp.pad(gain_local, ((0, 0), (0, HEAD_DIM - 4)))
    gain_all = jnp.tile(gain_pad, (1, ways))
    m_qkv = collect(spread_columns([w_query, w_key, w_value], ways))
    m_out = collect(spread_columns([jnp.transpose(w_out), gain_all], ways))
    m_gu = collect(spread_columns([w_gate, w_up], ways))
    m_down = collect(spread_columns([jnp.transpose(w_down)], ways))
    gains = jnp.transpose(m_out[:, own_feat:])[:8].astype(f32)
    m_out = m_out[:, :own_feat]
    gain_q = lax.dynamic_slice_in_dim(gains[0], me * own_feat, own_feat, 0)
    gain_k = lax.dynamic_slice_in_dim(gains[1], me * own_feat, own_feat, 0)
    x_row = gather_rows(token_rows)
    key_code = gather_rows(local_pos * 2 + key_ok)
    pos = key_code // 2
    qkv = dot_nn(x_row, m_qkv)
    q_raw, k_raw, v_raw = (qkv[:, i * own_feat : (i + 1) * own_feat] for i in range(3))
    squares = lax.psum(
        jnp.stack([jnp.sum(q_raw * q_raw, axis=-1), jnp.sum(k_raw * k_raw, axis=-1)]), "seq"
    )
    factors = lax.rsqrt(squares / feat_width + norm_eps)
    q_factor, k_factor = (factors[0][:, None], factors[1][:, None])
    cosine, sine = rope_tables(pos, HEAD_DIM)
    head_shape = (row_len, own_heads, HEAD_DIM)
    query_low = rotate((q_raw * q_factor * gain_q).reshape(head_shape), cosine, sine).astype(bf16)
    key_low = rotate((k_raw * k_factor * gain_k).reshape(head_shape), cosine, sine).astype(bf16)
    value_low = v_raw.astype(bf16).reshape(head_shape)
    mask = allowed_mask(pos, key_code)[None]
    scores = (
        jnp.einsum("qhd,khd->hqk", query_low, key_low, preferred_element_type=f32) * score_scale
    )
    expo = jnp.where(mask, jnp.exp(scores), 0.0)
    weight_sum = jnp.transpose(jnp.sum(expo, axis=-1))[:, :, None]
    expo_low = expo.astype(bf16)
    attn = jnp.einsum("hqk,khd->qhd", expo_low, value_low, preferred_element_type=f32) / weight_sum
    attn_low = attn.astype(bf16).reshape(row_len, own_feat)
    branch = scatter_rows(dot_nt(attn_low, m_out))
    branch_factor = rms_factor(branch)
    branch_unit = branch * branch_factor
    hidden_in = token_rows.astype(f32) + branch_unit * gains[2]
    hidden_low = gather_rows(hidden_in.astype(bf16))
    gate_up = dot_nn(hidden_low, m_gu)
    gate_val, up_val = (gate_up[:, :own_ff], gate_up[:, own_ff:])
    sigma = jax.nn.sigmoid(gate_val)
    mixed_low = (gate_val * sigma * up_val).astype(bf16)
    mlp_val = scatter_rows(dot_nt(mixed_low, m_down))
    mlp_factor = rms_factor(mlp_val)
    mlp_unit = mlp_val * mlp_factor
    layer_out = hidden_in + mlp_unit * gains[3]
    grad_gain_mlp = jnp.sum(grad_out * mlp_unit, axis=0)
    grad_mlp = gather_rows(norm_back(grad_out * gains[3], mlp_val, mlp_factor).astype(bf16))
    grad_mixed = dot_nn(grad_mlp, m_down)
    grad_gate = grad_mixed * up_val * sigma * (1.0 + gate_val * (1.0 - sigma))
    grad_up = grad_mixed * gate_val * sigma
    grad_gu = jnp.concatenate([grad_gate, grad_up], axis=1).astype(bf16)
    grad_hidden = grad_out + scatter_rows(dot_nt(grad_gu, m_gu))
    dw_gu = return_grads(dot_tn(hidden_low, grad_gu), [own_ff, own_ff], ways)
    dw_down = return_grads(dot_tn(grad_mlp, mixed_low), [own_ff], ways)
    grad_gain_attn = jnp.sum(grad_hidden * branch_unit, axis=0)
    grad_branch = gather_rows(norm_back(grad_hidden * gains[2], branch, branch_factor).astype(bf16))
    grad_attn = dot_nn(grad_branch, m_out).reshape(head_shape)
    dw_out = return_grads(dot_tn(grad_branch, attn_low), [own_feat], ways)
    grad_num = (grad_attn / weight_sum).astype(bf16)
    drop = jnp.transpose(jnp.sum(grad_attn * attn, axis=-1) / weight_sum[:, :, 0])
    grad_expo = jnp.einsum("qhd,khd->hqk", grad_num, value_low, preferred_element_type=f32)
    grad_scores = (expo * (grad_expo - drop[:, :, None])).astype(bf16)
    grad_q = (
        jnp.einsum("hqk,khd->qhd", grad_scores, key_low, preferred_element_type=f32) * score_scale
    )
    grad_k = (
        jnp.einsum("hqk,qhd->khd", grad_scores, query_low, preferred_element_type=f32) * score_scale
    )
    grad_v = jnp.einsum("hqk,qhd->khd", expo_low, grad_num, preferred_element_type=f32)
    grad_q_norm = unrotate(grad_q, cosine, sine).reshape(row_len, own_feat)
    grad_k_norm = unrotate(grad_k, cosine, sine).reshape(row_len, own_feat)
    q_unit, k_unit = (q_raw * q_factor, k_raw * k_factor)
    grad_gain_query = jnp.sum(grad_q_norm * q_unit, axis=0)
    grad_gain_key = jnp.sum(grad_k_norm * k_unit, axis=0)
    c_q, c_k = (grad_q_norm * gain_q, grad_k_norm * gain_k)
    means = (
        lax.psum(jnp.stack([jnp.sum(c_q * q_unit, axis=-1), jnp.sum(c_k * k_unit, axis=-1)]), "seq")
        / feat_width
    )
    grad_q_raw = q_factor * (c_q - q_unit * means[0][:, None])
    grad_k_raw = k_factor * (c_k - k_unit * means[1][:, None])
    grad_qkv = jnp.concatenate(
        [grad_q_raw, grad_k_raw, grad_v.reshape(row_len, own_feat)], axis=1
    ).astype(bf16)
    grad_tokens = grad_hidden + scatter_rows(dot_nt(grad_qkv, m_qkv))
    own_slot = jnp.zeros((2, feat_width), f32)
    own_slot = lax.dynamic_update_slice(
        own_slot, jnp.stack([grad_gain_query, grad_gain_key]), (0, me * own_feat)
    )
    gain_terms = jnp.concatenate([own_slot, jnp.stack([grad_gain_attn, grad_gain_mlp])])
    gain_columns = jnp.pad(jnp.transpose(gain_terms), ((0, 0), (0, HEAD_DIM - 4)))
    dw_qkv = return_grads(
        jnp.concatenate([dot_tn(x_row, grad_qkv), gain_columns], axis=1),
        [own_feat] * 3 + [HEAD_DIM],
        ways,
    )
    gain_grads = jnp.sum(dw_qkv[3].reshape(-1, ways, HEAD_DIM), axis=1)
    gain_grads = jnp.transpose(gain_grads[:, :8])
    return (
        layer_out.astype(bf16)[None],
        grad_tokens.astype(bf16)[None],
        dw_qkv[0],
        dw_qkv[1],
        dw_qkv[2],
        jnp.transpose(dw_out[0]),
        dw_gu[0],
        dw_gu[1],
        jnp.transpose(dw_down[0]),
        gain_grads[0],
        gain_grads[1],
        gain_grads[2],
        gain_grads[3],
    )


def solution(mesh):
    both = ("dp", "seq")
    in_specs = (
        P("dp", "seq", None),
        P(both, None),
        P(both, None),
        P(both, None),
        P(None, both),
        P(both, None),
        P(both, None),
        P(None, both),
        P(both),
        P(both),
        P(both),
        P(both),
        P("dp", "seq", None),
        P("dp", "seq"),
        P("dp"),
        P("dp", "seq"),
    )
    out_specs = (
        P("dp", "seq", None),
        P("dp", "seq", None),
        P(both, None),
        P(both, None),
        P(both, None),
        P(None, both),
        P(both, None),
        P(both, None),
        P(None, both),
        P(both),
        P(both),
        P(both),
        P(both),
    )
    return jax.shard_map(body, mesh=mesh, in_specs=in_specs, out_specs=out_specs, check_vma=False)
```

profile of v0, /device:TPU:9, one launch (start us, length us, event | category | flops | bytes accessed | tf_op | source)
XLA Modules:
  0.0 1109.0 jit_solution(11077632735175738909)
XLA Ops:
  9.3 15.8 %all_to_all.125 = bf16[64,8,384]{2,0,1:T(8,128)(2,1)} all-to-all(bf16[64,8,384]{2,0,1:T(8,128)(2,1)S(1)} %copy.115), channel_id=1, replica_groups=mesh['dp'=4,'seq'=8] {'seq'}, dimensions={1} | all-to-all | bytes 786432 | tf_op jit(solution)/shard_map/all_to_all | solution.py:73
  25.6 23.3 %all_to_all.126 = bf16[64,8,768]{2,0,1:T(8,128)(2,1)} all-to-all(bf16[64,8,768]{2,0,1:T(8,128)(2,1)S(1)} %copy.113), channel_id=1, replica_groups=mesh['dp'=4,'seq'=8] {'seq'}, dimensions={1} | all-to-all | bytes 1572864 | tf_op jit(solution)/shard_map/all_to_all | solution.py:73
  53.6 6.9 all-reduce.2
  60.7 3.3 broadcast_multiply_fusion.3
  64.0 2.8 or_and_fusion
  68.0 1.4 slice_reduce_fusion
  69.7 32.8 %all-gather.10.cloned.1.call-done = bf16[2048,768]{1,0:T(8,128)(2,1)} async-done(((bf16[512,768]{1,0:T(8,128)(2,1)}), bf16[2048,768]{1,0:T(8,128)(2,1)}) %all-gather.10.cloned.1.call-update) | async-done | bytes 3145744 | tf_op jit(solution)/shard_map/all_gather | solution.py:74
  102.5 56.4 %all-gather.24.cloned.1.call-done = bf16[1,1280,2048]{2,1,0:T(8,128)(2,1)} async-done(((bf16[1,160,2048]{2,1,0:T(8,128)(2,1)}), bf16[1,1280,2048]{2,1,0:T(8,128)(2,1)}) %all-gather.24.cloned.1.call-update) | async-done | bytes 5242896 | tf_op jit(solution)/shard_map/all_gather | solution.py:78
  158.9 7.7 fusion.7
  166.8 1.7 copy-done.1
  168.6 22.2 %psum.14 = f32[2,1280]{1,0:T(2,128)S(1)} all-reduce(f32[2,1280]{1,0:T(2,128)S(1)} %pad_maximum_fusion.10), channel_id=1, replica_groups=mesh['dp'=4,'seq'=8] {'seq'}, use_global_device_ids=true, to_apply=%region_2.3 | all-reduce | flops 2560 | bytes 20480 | tf_op jit(solution)/shard_map/psum | solution.py:152
  190.9 2.0 fusion.63
  194.5 3.5 fusion.83
  198.1 2.2 fusion.84
  200.3 3.1 copy-done
  204.2 3.8 convolution_convert_fusion.4
  211.9 88.8 %all_to_all.127 = bf16[64,8,2048]{2,0,1:T(8,128)(2,1)} all-to-all(bf16[64,8,2048]{2,0,1:T(8,128)(2,1)S(1)} %copy.119), channel_id=1, replica_groups=mesh['dp'=4,'seq'=8] {'seq'}, dimensions={1} | all-to-all | bytes 4194304 | tf_op jit(solution)/shard_map/all_to_all | solution.py:73
  300.8 15.4 %reduce-scatter.9.cloned.1.call-done = bf16[160,2048]{1,0:T(8,128)(2,1)} async-done(((bf16[1280,2048]{1,0:T(8,128)(2,1)}), bf16[160,2048]{1,0:T(8,128)(2,1)}) %reduce-scatter.9.cloned.1.call-update) | async-done | bytes 655376 | tf_op jit(solution)/shard_map/reduce_scatter | solution.py:82
  317.5 2.2 fusion.58
  319.9 27.2 %all_to_all.128 = bf16[64,8,1024]{2,0,1:T(8,128)(2,1)} all-to-all(bf16[64,8,1024]{2,0,1:T(8,128)(2,1)S(1)} %bitcast.187), channel_id=1, replica_groups=mesh['dp'=4,'seq'=8] {'seq'}, dimensions={1} | all-to-all | bytes 2097152 | tf_op jit(solution)/shard_map/all_to_all | solution.py:73
  347.6 57.2 %all-gather.16.cloned.1.call-done = bf16[2048,2048]{1,0:T(8,128)(2,1)} async-done(((bf16[512,2048]{1,0:T(8,128)(2,1)}), bf16[2048,2048]{1,0:T(8,128)(2,1)}) %all-gather.16.cloned.1.call-update) | async-done | bytes 8388624 | tf_op jit(solution)/shard_map/all_gather | solution.py:74
  404.9 56.8 %all-gather.14.cloned.1.call-done = bf16[1280,2048]{1,0:T(8,128)(2,1)} async-done(((bf16[160,2048]{1,0:T(8,128)(2,1)}), bf16[1280,2048]{1,0:T(8,128)(2,1)}) %all-gather.14.cloned.1.call-update) | async-done | bytes 5242896 | tf_op jit(solution)/shard_map/all_gather | solution.py:78
  461.7 15.2 %fusion.85 = f32[1280,2048]{1,0:T(8,128)S(1)} fusion(bf16[1280,2048]{1,0:T(8,128)(2,1)} %all-gather.14.cloned.1.call-done, bf16[2048,2048]{1,0:T(8,128)(2,1)} %all-gather.16.cloned.1.call-done), kind=kOutput, calls=%fused_computation.180 | convolution fusion | flops 10737418240 | bytes 24117248 | tf_op jit(solution)/shard_map/dot_general | solution.py:54
  476.9 3.9 copy-done.5
  480.8 2.7 multiply_convert_fusion.2
  483.5 32.9 %all-gather.18.cloned.1.call-done = bf16[2048,1024]{1,0:T(8,128)(2,1)} async-done(((bf16[512,1024]{1,0:T(8,128)(2,1)}), bf16[2048,1024]{1,0:T(8,128)(2,1)}) %all-gather.18.cloned.1.call-update) | async-done | bytes 4194320 | tf_op jit(solution)/shard_map/all_gather | solution.py:74
  516.4 9.9 convolution_convert_fusion.3
  526.4 58.5 %reduce-scatter.11.cloned.1.call-done = bf16[160,2048]{1,0:T(8,128)(2,1)} async-done(((bf16[1280,2048]{1,0:T(8,128)(2,1)}), bf16[160,2048]{1,0:T(8,128)(2,1)}) %reduce-scatter.11.cloned.1.call-update) | async-done | bytes 655376 | tf_op jit(solution)/shard_map/reduce_scatter | solution.py:82
  586.2 1.7 fusion.51
  589.4 54.5 %all-gather.20.cloned.1.call-done = bf16[1280,2048]{1,0:T(8,128)(2,1)} async-done(((bf16[160,2048]{1,0:T(8,128)(2,1)}), bf16[1280,2048]{1,0:T(8,128)(2,1)}) %all-gather.20.cloned.1.call-update) | async-done | bytes 5242896 | tf_op jit(solution)/shard_map/all_gather | solution.py:78
  643.9 13.1 %multiply_convert_fusion.1 = (bf16[1280,1024]{1,0:T(8,128)(2,1)S(1)}, bf16[1280,1024]{1,0:T(8,128)(2,1)S(1)}) fusion(f32[1280,2048]{1,0:T(8,128)} %copy-done.5, bf16[1280,2048]{1,0:T(8,128)(2,1)} %all-gather.20.cloned.1.call-done, bf16[2048,1024]{1,0:T(8,128)(2,1)} %all-gather.18.cloned.1.call-done), kind=kOutput, calls=%fused_computation.19 | convolution fusion | flops 5385748480 | bytes 25165824 | tf_op jit(solution)/shard_map/dot_general | solution.py:54
  657.1 1.6 copy-done.41
  659.3 15.3 %convolution_convert_fusion.2 = bf16[1280,2048]{1,0:T(8,128)(2,1)} fusion(bf16[2048,2048]{1,0:T(8,128)(2,1)} %all-gather.16.cloned.1.call-done, bf16[1280,1024]{1,0:T(8,128)(2,1)S(1)} %get-tuple-element.38, bf16[1280,1024]{1,0:T(8,128)(2,1)S(1)} %get-tuple-element.37), kind=kOutput, calls=%fused_computation.7 | convolution fusion | flops 10750525440 | bytes 18874368 | tf_op jit(solution)/shard_map/dot_general | solution.py:58
  674.7 58.6 %reduce-scatter.13.cloned.1.call-done = bf16[160,2048]{1,0:T(8,128)(2,1)} async-done(((bf16[1280,2048]{1,0:T(8,128)(2,1)}), bf16[160,2048]{1,0:T(8,128)(2,1)}) %reduce-scatter.13.cloned.1.call-update) | async-done | bytes 655376 | tf_op jit(solution)/shard_map/reduce_scatter | solution.py:82
  733.4 1.8 fusion.45
  735.2 1.9 fusion.44
  737.1 10.2 convolution_convert_fusion.5
  747.6 16.7 %convolution_convert_fusion = bf16[2048,2048]{1,0:T(8,128)(2,1)} fusion(bf16[1280,2048]{1,0:T(8,128)(2,1)} %all-gather.14.cloned.1.call-done, bf16[1280,1024]{1,0:T(8,128)(2,1)} %copy-done.42, bf16[1280,1024]{1,0:T(8,128)(2,1)} %copy-done.41), kind=kOutput, calls=%fused_computation.5 | convolution fusion | flops 10752098304 | bytes 18874368 | tf_op jit(solution)/shard_map/dot_general | solution.py:62
  764.4 27.4 %all-gather.22.cloned.1.call-done = bf16[1280,2048]{1,0:T(8,128)(2,1)} async-done(((bf16[160,2048]{1,0:T(8,128)(2,1)}), bf16[1280,2048]{1,0:T(8,128)(2,1)}) %all-gather.22.cloned.1.call-update) | async-done | bytes 5242896 | tf_op jit(solution)/shard_map/all_gather | solution.py:78
  791.8 4.7 multiply_reduce_fusion.2
  796.6 6.3 fusion.1
  802.9 2.2 convolution_bitcast_fusion
  807.9 1.7 copy-done.2
  810.4 23.1 %psum.15 = f32[2,1280]{1,0:T(2,128)S(1)} all-reduce(f32[2,1280]{1,0:T(2,128)S(1)} %pad_maximum_fusion.11), channel_id=1, replica_groups=mesh['dp'=4,'seq'=8] {'seq'}, use_global_device_ids=true, to_apply=%region_14.15 | all-reduce | flops 2560 | bytes 20480 | tf_op jit(solution)/shard_map/psum | solution.py:215
  833.6 5.3 convolution_convert_fusion.6
  839.0 2.6 multiply_convert_fusion.4
  841.7 7.5 fusion.27
  849.2 5.6 fusion.18
  854.8 2.3 fusion.10
  858.7 8.0 convolution_convert_fusion.1
  866.7 33.6 %all_to_all.129 = bf16[8,64,1024]{2,1,0:T(8,128)(2,1)} all-to-all(bf16[8,64,1024]{2,1,0:T(8,128)(2,1)} %bitcast.201), channel_id=1, replica_groups=mesh['dp'=4,'seq'=8] {'seq'}, dimensions={0} | all-to-all | bytes 2097152 | tf_op jit(solution)/shard_map/all_to_all | solution.py:90
  900.3 36.9 %reduce-scatter.21.cloned.1.call-done = bf16[512,2048]{1,0:T(8,128)(2,1)} async-done(((bf16[2048,2048]{1,0:T(8,128)(2,1)}), bf16[512,2048]{1,0:T(8,128)(2,1)}) %reduce-scatter.21.cloned.1.call-update) | async-done | bytes 2097168 | tf_op jit(solution)/shard_map/reduce_scatter | solution.py:88
  937.2 51.5 %all_to_all.130 = bf16[8,64,2048]{2,1,0:T(8,128)(2,1)S(1)} all-to-all(bf16[8,64,2048]{2,1,0:T(8,128)(2,1)} %bitcast.192), channel_id=1, replica_groups=mesh['dp'=4,'seq'=8] {'seq'}, dimensions={0} | all-to-all | bytes 4194304 | tf_op jit(solution)/shard_map/all_to_all | solution.py:90
  988.7 6.3 all-to-all-start.5
  995.1 24.7 %reduce-scatter.17.cloned.1.call-done = bf16[512,896]{0,1:T(8,128)(2,1)} async-done(((bf16[2048,896]{0,1:T(8,128)(2,1)}), bf16[512,896]{0,1:T(8,128)(2,1)}) %reduce-scatter.17.cloned.1.call-update) | async-done | bytes 917520 | tf_op jit(solution)/shard_map/reduce_scatter | solution.py:88
  1019.8 2.2 copy.129
  1022.0 5.5 all-to-all-start.4
  1027.4 1.5 convert_bitcast_fusion
  1029.0 1.5 copy.155
  1030.9 1.5 copy.153
  1032.3 1.5 copy.154
  1034.7 26.6 %all-to-all-done.4 = bf16[8,64,896]{2,1,0:T(8,128)(2,1)} async-done(((bf16[8,64,896]{2,1,0:T(8,128)(2,1)}), bf16[8,64,896]{2,1,0:T(8,128)(2,1)}, u32[]{:S(2)}, u32[]{:S(2)}) %all-to-all-start.4) | async-done | bytes 917536 | tf_op jit(solution)/shard_map/all_to_all | solution.py:90
  1066.8 33.0 %reduce-scatter.15.cloned.1.call-done = bf16[160,2048]{1,0:T(8,128)(2,1)} async-done(((bf16[1280,2048]{1,0:T(8,128)(2,1)}), bf16[160,2048]{1,0:T(8,128)(2,1)}) %reduce-scatter.15.cloned.1.call-update) | async-done | bytes 655376 | tf_op jit(solution)/shard_map/reduce_scatter | solution.py:82
  1099.8 2.2 fusion.64
  (194 shorter events, 32.2 us)
Async XLA Ops:
  7.2 18.0 %copy-start.27 = (bf16[64,2048]{1,0:T(8,128)(2,1)S(1)}, bf16[64,2048]{1,0:T(8,128)(2,1)}, u32[]{:S(2)}) copy-start(bf16[64,2048]{1,0:T(8,128)(2,1)} %param.17) | copy-start | bytes 786436
  7.2 18.1 %copy-start.28 = (bf16[64,2048]{1,0:T(8,128)(2,1)S(1)}, bf16[64,2048]{1,0:T(8,128)(2,1)}, u32[]{:S(2)}) copy-start(bf16[64,2048]{1,0:T(8,128)(2,1)} %param.18) | copy-start | bytes 786436
  7.2 59.6 %all-gather.12.cloned.1.call-start = ((), (), s32[]{:S(2)}) async-start(), calls=%async_computation.17 | async-start | bytes 1966080 | tf_op jit(solution)/shard_map/all_gather | solution.py:74
  8.3 17.0 %copy-start.29 = (bf16[64,2048]{1,0:T(8,128)(2,1)S(1)}, bf16[64,2048]{1,0:T(8,128)(2,1)}, u32[]{:S(2)}) copy-start(bf16[64,2048]{1,0:T(8,128)(2,1)} %param.19) | copy-start | bytes 786436
  25.1 77.4 %all-gather.10.cloned.1.call-start = ((), (), s32[]{:S(2)}) async-start(), calls=%async_computation.16 | async-start | bytes 3932160 | tf_op jit(solution)/shard_map/all_gather | solution.py:74
  25.4 24.9 %copy-start.40 = (u32[32]{0:T(128)S(1)}, u32[32]{0:T(128)}, u32[]{:S(2)}) copy-start(u32[32]{0:T(128)} %constant.93) | copy-start | bytes 388
  25.5 26.1 %copy-start.38 = (s32[1,2]{1,0:T(1,128)S(1)}, s32[1,2]{1,0:T(1,128)}, u32[]{:S(2)}) copy-start(s32[1,2]{1,0:T(1,128)} %param.31) | copy-start | bytes 28
  25.5 26.7 %copy-start.39 = (s32[1,160]{1,0:T(1,128)S(1)}, s32[1,160]{1,0:T(1,128)}, u32[]{:S(2)}) copy-start(s32[1,160]{1,0:T(1,128)} %param.29) | copy-start | bytes 1924
  48.9 109.9 %all-gather.24.cloned.1.call-start = ((), (), s32[]{:S(2)}) async-start(), calls=%async_computation.31 | async-start | bytes 5898240 | tf_op jit(solution)/shard_map/all_gather | solution.py:78
  49.7 266.6 %reduce-scatter.9.cloned.1.call-start = ((), (), s32[]{:S(2)}) async-start(), calls=%async_computation.18 | async-start | bytes 5898240 | tf_op jit(solution)/shard_map/reduce_scatter | solution.py:82
  69.6 121.2 %copy-start.34 = (f32[256]{0:T(256)}, f32[256]{0:T(256)S(1)}, u32[]{:S(2)}) copy-start(f32[256]{0:T(256)S(1)} %get-tuple-element.79) | copy-start | bytes 3076
  69.6 121.2 %copy-start.36 = (f32[256]{0:T(256)}, f32[256]{0:T(256)S(1)}, u32[]{:S(2)}) copy-start(f32[256]{0:T(256)S(1)} %get-tuple-element.80) | copy-start | bytes 3076
  166.6 1.9 copy-start.1
  190.8 2.0 copy-start.30
  190.9 2.0 copy-start.32
  193.1 1.4 copy-start.18
  193.7 4.4 copy-start.16
  198.1 5.3 copy-start
  198.1 6.1 copy-start.19
  203.4 0.8 copy-start.14
  208.1 1.2 copy-start.20
  208.1 196.8 %all-gather.16.cloned.1.call-start = ((), (), s32[]{:S(2)}) async-start(), calls=%async_computation.20 | async-start | bytes 10485760 | tf_op jit(solution)/shard_map/all_gather | solution.py:74
  208.1 1.8 copy-start.21
  300.7 16.8 %copy-start.10 = (bf16[1,160,2048]{2,1,0:T(8,128)(2,1)S(1)}, bf16[1,160,2048]{2,1,0:T(8,128)(2,1)}, u32[]{:S(2)}) copy-start(bf16[1,160,2048]{2,1,0:T(8,128)(2,1)} %param.16) | copy-start | bytes 1966084
  300.7 19.1 %copy-start.22 = (bf16[8192,64]{0,1:T(8,128)(2,1)S(1)}, bf16[8192,64]{0,1:T(8,128)(2,1)}, u32[]{:S(2)}) copy-start(bf16[8192,64]{0,1:T(8,128)(2,1)} %param.23) | copy-start | bytes 3145732
  300.7 160.9 %all-gather.14.cloned.1.call-start = ((), (), s32[]{:S(2)}) async-start(), calls=%async_computation.19 | async-start | bytes 5898240 | tf_op jit(solution)/shard_map/all_gather | solution.py:78
  319.8 196.6 %all-gather.18.cloned.1.call-start = ((), (), s32[]{:S(2)}) async-start(), calls=%async_computation.21 | async-start | bytes 5242880 | tf_op jit(solution)/shard_map/all_gather | solution.py:74
  347.2 237.7 %reduce-scatter.11.cloned.1.call-start = ((), (), s32[]{:S(2)}) async-start(), calls=%async_computation.22 | async-start | bytes 5898240 | tf_op jit(solution)/shard_map/reduce_scatter | solution.py:82
  476.9 3.9 copy-start.5
  526.3 60.0 %copy-start.3 = (bf16[1,160,2048]{2,1,0:T(8,128)(2,1)S(1)}, bf16[1,160,2048]{2,1,0:T(8,128)(2,1)}, u32[]{:S(2)}) copy-start(bf16[1,160,2048]{2,1,0:T(8,128)(2,1)} %param.28) | copy-start | bytes 1966084
  526.3 117.6 %all-gather.20.cloned.1.call-start = ((), (), s32[]{:S(2)}) async-start(), calls=%async_computation.23 | async-start | bytes 5898240 | tf_op jit(solution)/shard_map/all_gather | solution.py:78
  584.9 3.1 copy-start.6
  589.2 144.2 %reduce-scatter.13.cloned.1.call-start = ((), (), s32[]{:S(2)}) async-start(), calls=%async_computation.24 | async-start | bytes 5898240 | tf_op jit(solution)/shard_map/reduce_scatter | solution.py:82
  657.1 1.6 copy-start.41
  657.1 2.3 copy-start.42
  674.6 58.7 %copy-start.4 = (bf16[160,2048]{1,0:T(8,128)(2,1)S(1)}, bf16[160,2048]{1,0:T(8,128)(2,1)}, u32[]{:S(2)}) copy-start(bf16[160,2048]{1,0:T(8,128)(2,1)} %reduce-scatter.9.cloned.1.call-done) | copy-start | bytes 1966084
  674.7 117.1 %all-gather.22.cloned.1.call-start = ((), (), s32[]{:S(2)}) async-start(), calls=%async_computation.25 | async-start | bytes 5898240 | tf_op jit(solution)/shard_map/all_gather | solution.py:78
  733.4 1.8 copy-start.8
  733.4 1.8 copy-start.11
  737.1 129.6 %reduce-scatter.23.cloned.1.call-start = ((), (), s32[]{:S(2)}) async-start(), calls=%async_computation.30 | async-start | bytes 5242880 | tf_op jit(solution)/shard_map/reduce_scatter | solution.py:88
  747.3 189.9 %reduce-scatter.21.cloned.1.call-start = ((), (), s32[]{:S(2)}) async-start(), calls=%async_computation.29 | async-start | bytes 10485760 | tf_op jit(solution)/shard_map/reduce_scatter | solution.py:88
  764.3 224.5 %reduce-scatter.19.cloned.1.call-start = ((), (), s32[]{:S(2)}) async-start(), calls=%async_computation.28 | async-start | bytes 1310720 | tf_op jit(solution)/shard_map/reduce_scatter | solution.py:88
  796.5 6.4 copy-start.12
  796.5 6.3 copy-start.17
  802.9 2.2 copy-start.7
  806.4 1.1 copy-start.15
  807.5 2.1 copy-start.2
  807.5 2.1 copy-start.31
  807.5 2.2 copy-start.33
  807.5 2.2 copy-start.35
  807.5 2.1 copy-start.37
  838.9 180.8 %reduce-scatter.17.cloned.1.call-start = ((), (), s32[]{:S(2)}) async-start(), calls=%async_computation.27 | async-start | bytes 4587520 | tf_op jit(solution)/shard_map/reduce_scatter | solution.py:88
  839.0 2.7 copy-start.13
  839.0 10.2 slice-start
  841.6 7.6 copy-start.23
  841.6 7.6 copy-start.25
  841.7 7.5 slice-start.1
  857.1 1.2 copy-start.24
  857.1 1.6 copy-start.26
  857.1 242.6 %reduce-scatter.15.cloned.1.call-start = ((), (), s32[]{:S(2)}) async-start(), calls=%async_computation.26 | async-start | bytes 5898240 | tf_op jit(solution)/shard_map/reduce_scatter | solution.py:82
  988.7 33.2 %all-to-all-start.5 = ((bf16[8,64,256]{2,1,0:T(8,128)(2,1)}), bf16[8,64,256]{2,1,0:T(8,128)(2,1)S(1)}, u32[]{:S(2)}, u32[]{:S(2)}) async-start(bf16[8,64,256]{2,1,0:T(8,128)(2,1)} %bitcast.218), calls=%async_computation.11 | async-start | bytes 524288 | tf_op jit(solution)/shard_map/all_to_all | solution.py:90
  1022.0 39.3 %all-to-all-start.4 = ((bf16[8,64,896]{2,1,0:T(8,128)(2,1)}), bf16[8,64,896]{2,1,0:T(8,128)(2,1)}, u32[]{:S(2)}, u32[]{:S(2)}) async-start(bf16[8,64,896]{2,1,0:T(8,128)(2,1)} %bitcast.190), calls=%async_computation.9 | async-start | bytes 1835008 | tf_op jit(solution)/shard_map/all_to_all | solution.py:90
  1062.5 37.2 %copy-start.9 = (bf16[160,2048]{1,0:T(8,128)(2,1)S(1)}, bf16[160,2048]{1,0:T(8,128)(2,1)}, u32[]{:S(2)}) copy-start(bf16[160,2048]{1,0:T(8,128)(2,1)} %reduce-scatter.13.cloned.1.call-done) | copy-start | bytes 1966084
Sparse Core Ops, SparseCore 0:
  25.2 31.3 all-gather.11
  58.5 43.9 all-gather.9
  104.1 54.6 all-gather.23
  208.2 107.9 reduce-scatter.8
  317.9 86.8 all-gather.15
  406.9 54.6 all-gather.13
  463.5 52.8 all-gather.17
  526.4 58.3 reduce-scatter.10
  589.3 54.5 all-gather.19
  674.8 58.5 reduce-scatter.12
  737.2 54.5 all-gather.21
  794.6 52.8 reduce-scatter.22
  850.8 86.3 reduce-scatter.20
  940.5 27.7 reduce-scatter.18
  971.4 48.3 reduce-scatter.16
  1022.0 77.6 reduce-scatter.14
where the time goes:
time: 1120 us; the launch traced here: 1110 us
  waiting for transfers between devices  573 us (51%)
  blocking collectives  292 us (26%)
  matrix products  138 us (12%)
  other arithmetic  38.8 us (3%)
  local copies, waits for them, and re-layouts  36.8 us (3%)
  between operations  16.6 us (1%)
  starting transfers between devices  13.3 us (1%)
    all_gather x4, waiting for transfers between devices, gather_rows(): return lax.all_gather(rows, 'seq', axis=0, tiled=True)  195 us
    reduce_scatter x4, waiting for transfers between devices, scatter_rows(): lax.psum_scatter(partial_rows.astype(bf16), 'seq', scatter_dimension=0, t...  166 us
    all_to_all x4, blocking collectives, collect(): lax.all_to_all(matrix, 'seq', split_axis=1, concat_axis=0, tiled=True)  155 us
    all_gather x4, waiting for transfers between devices, collect(): return lax.all_gather(moved, 'dp', axis=0, tiled=True)  123 us
    all_to_all x2, blocking collectives, return_grads(): lax.all_to_all(summed, 'seq', split_axis=0, concat_axis=1, tiled=True)  85.1 us
    reduce_scatter x4, waiting for transfers between devices, return_grads(): lax.psum_scatter(grad.astype(bf16), 'dp', scatter_dimension=0, tiled=True)  61.6 us
    dot_general x4, matrix products, dot_nn(): return jnp.dot(left, right, preferred_element_type=f32)  40.8 us
    dot_general x4, matrix products, dot_tn(): lax.dot_general(left, right, (((0,), (0,)), ((), ())), preferred_element_...  37.7 us
  transfers between devices with their start and end apart: 18, of which 14 were waited for; matrix products, arithmetic and copies ran while one was open for 11% of the time, Pallas kernels for 0%

commit v1 on v0

--- a/solution.py
+++ b/solution.py
@@ -71,7 +71,23 @@
 
 def collect(matrix):
     moved = lax.all_to_all(matrix, "seq", split_axis=1, concat_axis=0, tiled=True)
-    return lax.all_gather(moved, "dp", axis=0, tiled=True)
+
+    def _apply_set(field_in, row_axis):
+        everything = lax.axis_size(row_axis)
+        long_array = lax.axis_index(row_axis)
+        g_now, main, local_now = (everything, long_array, field_in.shape[0])
+        value_now, plain = (field_in, 1)
+        while plain < g_now:
+            reached = lax.ppermute(
+                value_now,
+                axis_name=row_axis,
+                perm=[(rr, (rr - plain) % g_now) for rr in range(g_now)],
+            )
+            value_now = jnp.concatenate([value_now, reached], 0)
+            plain = 2 * plain
+        return jnp.roll(value_now, main * local_now, 0)
+
+    return _apply_set(moved, "dp")
 
 
 def gather_rows(rows):

time: 1120 us -> 1170 us (1.045)
  blocking collectives: 292 us -> 198 us
  waiting for transfers between devices: 573 us -> 650 us
  starting transfers between devices: 13.3 us -> 56.8 us
  local copies, waits for them, and re-layouts: 36.8 us -> 61.5 us
    ppermute x0 -> x8, waiting for transfers between devices: none -> 171 us  [_apply_set(): lax.ppermute(value_now, axis_name=row_axis, perm=[(rr, (rr - plain) % g_n...]
    all_gather x4 -> x0, waiting for transfers between devices: 123 us -> none  [collect(): return lax.all_gather(moved, 'dp', axis=0, tiled=True)]
    all_gather x4, waiting for transfers between devices: 195 us -> 81.6 us  [gather_rows(): return lax.all_gather(rows, 'seq', axis=0, tiled=True)]
    reduce_scatter x4, waiting for transfers between devices: 166 us -> 275 us  [scatter_rows(): lax.psum_scatter(partial_rows.astype(bf16), 'seq', scatter_dimension=0, t...]
    all_to_all x4 -> x1, blocking collectives: 155 us -> 53.2 us  [collect(): lax.all_to_all(matrix, 'seq', split_axis=1, concat_axis=0, tiled=True)]
    all_to_all x0 -> x3, waiting for transfers between devices: none -> 33 us  [collect(): lax.all_to_all(matrix, 'seq', split_axis=1, concat_axis=0, tiled=True)]
    all_to_all x0 -> x3, starting transfers between devices: none -> 22.1 us  [collect(): lax.all_to_all(matrix, 'seq', split_axis=1, concat_axis=0, tiled=True)]
    ppermute x0 -> x8, starting transfers between devices: none -> 21.6 us  [_apply_set(): lax.ppermute(value_now, axis_name=row_axis, perm=[(rr, (rr - plain) % g_n...]
  transfers between devices with their start and end apart: 18 -> 25, of which waited for: 14 -> 15; matrix products, arithmetic and copies ran while one was open for 11% -> 11% of each run, Pallas kernels for 0% -> 0%
where the time goes in v1:
time: 1170 us; the launch traced here: 1160 us
  waiting for transfers between devices  650 us (56%)
  blocking collectives  198 us (17%)
  matrix products  140 us (12%)
  local copies, waits for them, and re-layouts  61.5 us (5%)
  starting transfers between devices  56.8 us (5%)
  other arithmetic  41 us (4%)
  between operations  17 us (1%)
    reduce_scatter x4, waiting for transfers between devices, scatter_rows(): lax.psum_scatter(partial_rows.astype(bf16), 'seq', scatter_dimension=0, t...  275 us
    ppermute x8, waiting for transfers between devices, _apply_set(): lax.ppermute(value_now, axis_name=row_axis, perm=[(rr, (rr - plain) % g_n...  171 us
    all_to_all x2, blocking collectives, return_grads(): lax.all_to_all(summed, 'seq', split_axis=0, concat_axis=1, tiled=True)  85 us
    all_gather x4, waiting for transfers between devices, gather_rows(): return lax.all_gather(rows, 'seq', axis=0, tiled=True)  81.6 us
    reduce_scatter x4, waiting for transfers between devices, return_grads(): lax.psum_scatter(grad.astype(bf16), 'dp', scatter_dimension=0, tiled=True)  61.7 us
    all_to_all x1, blocking collectives, collect(): lax.all_to_all(matrix, 'seq', split_axis=1, concat_axis=0, tiled=True)  53.2 us
    dot_general x4, matrix products, dot_nn(): return jnp.dot(left, right, preferred_element_type=f32)  40.5 us
    unnamed x119, local copies, waits for them, and re-layouts  39 us
  transfers between devices with their start and end apart: 25, of which 15 were waited for; matrix products, arithmetic and copies ran while one was open for 11% of the time, Pallas kernels for 0%

profile of v1, /device:TPU:9, one launch (start us, length us, event | category | flops | bytes accessed | tf_op | source)
XLA Modules:
  0.0 1164.6 jit_solution(1013503327694734546)
XLA Ops:
  10.7 5.6 all-to-all-start.1
  21.6 12.5 %all-reduce.2 = s32[1280]{0:T(1024)S(1)} all-reduce(s32[1280]{0:T(1024)S(1)} %fusion.90), channel_id=1, replica_groups=mesh['dp'=4,'seq'=8] {'seq'}, use_global_device_ids=true, to_apply=%add.2 | all-reduce | flops 1280 | bytes 10240
  34.1 6.8 all-to-all-start
  40.9 2.8 or_and_fusion
  43.7 2.2 collective-permute-start.2
  46.0 33.0 %all-to-all-done = bf16[64,8,768]{2,0,1:T(8,128)(2,1)S(1)} async-done(((bf16[64,8,768]{2,0,1:T(8,128)(2,1)}), bf16[64,8,768]{2,0,1:T(8,128)(2,1)S(1)}, u32[]{:S(2)}, u32[]{:S(2)}) %all-to-all-start) | async-done | bytes 786464 | tf_op jit(solution)/shard_map/all_to_all | solution.py:73
  79.0 2.2 collective-permute-start
  81.5 3.5 broadcast_multiply_fusion.3
  86.1 11.6 collective-permute-done
  104.5 28.6 %collective-permute-done.1 = bf16[1024,768]{1,0:T(8,128)(2,1)S(1)} collective-permute-done((bf16[1024,768]{1,0:T(8,128)(2,1)S(1)}, bf16[1024,768]{1,0:T(8,128)(2,1)S(1)}, u32[]{:S(2)}, u32[]{:S(2)}) %collective-permute-start.1) | collective-permute-done | bytes 1572896 | tf_op jit(solution)/shard_map/ppermute | solution.py:81
  137.5 7.7 fusion.10
  147.2 25.0 %psum.14 = f32[2,1280]{1,0:T(2,128)S(1)} all-reduce(f32[2,1280]{1,0:T(2,128)S(1)} %pad_maximum_fusion.14), channel_id=1, replica_groups=mesh['dp'=4,'seq'=8] {'seq'}, use_global_device_ids=true, to_apply=%region_2.3 | all-reduce | flops 2560 | bytes 20480 | tf_op jit(solution)/shard_map/psum | solution.py:168
  172.3 2.0 fusion.71
  177.1 3.5 fusion.99
  180.6 2.7 fusion.100
  183.4 2.3 copy-done
  186.5 5.1 convolution_convert_fusion.4
  194.3 2.5 copy.119
  196.8 9.7 all-to-all-start.2
  206.4 97.6 %reduce-scatter.9.cloned.1.call-done = bf16[160,2048]{1,0:T(8,128)(2,1)} async-done(((bf16[1280,2048]{1,0:T(8,128)(2,1)}), bf16[160,2048]{1,0:T(8,128)(2,1)}) %reduce-scatter.9.cloned.1.call-update) | async-done | bytes 655376 | tf_op jit(solution)/shard_map/reduce_scatter | solution.py:98
  305.3 2.4 fusion.66
  307.9 12.4 %collective-permute-start.4 = (bf16[512,2048]{1,0:T(8,128)(2,1)S(1)}, bf16[512,2048]{1,0:T(8,128)(2,1)S(1)}, u32[]{:S(2)}, u32[]{:S(2)}) collective-permute-start(bf16[512,2048]{1,0:T(8,128)(2,1)S(1)} %bitcast.168), channel_id=1, source_target_pairs={{0,24},{8,0},{16,8},{24,16},{1,25},{9,1},{17,9},{25,17},{2,26},{10... | collective-permute-start | bytes 6291464 | tf_op jit(solution)/shard_map/ppermute | solution.py:81
  321.6 53.2 %all_to_all.125 = bf16[64,8,1024]{2,0,1:T(8,128)(2,1)S(1)} all-to-all(bf16[64,8,1024]{2,0,1:T(8,128)(2,1)S(1)} %bitcast.193), channel_id=1, replica_groups=mesh['dp'=4,'seq'=8] {'seq'}, dimensions={1} | all-to-all | bytes 2097152 | tf_op jit(solution)/shard_map/all_to_all | solution.py:73
  376.0 21.2 %collective-permute-done.6 = bf16[512,1024]{1,0:T(8,128)(2,1)S(1)} collective-permute-done((bf16[512,1024]{1,0:T(8,128)(2,1)S(1)}, bf16[512,1024]{1,0:T(8,128)(2,1)S(1)}, u32[]{:S(2)}, u32[]{:S(2)}) %collective-permute-start.6) | collective-permute-done | bytes 1048608 | tf_op jit(solution)/shard_map/ppermute | solution.py:81
  397.4 2.6 collective-permute-start.7
  401.6 108.6 %collective-permute-done.7 = bf16[1024,1024]{1,0:T(8,128)(2,1)S(1)} collective-permute-done((bf16[1024,1024]{1,0:T(8,128)(2,1)S(1)}, bf16[1024,1024]{1,0:T(8,128)(2,1)S(1)}, u32[]{:S(2)}, u32[]{:S(2)}) %collective-permute-start.7) | collective-permute-done | bytes 2097184 | tf_op jit(solution)/shard_map/ppermute | solution.py:81
  510.7 1.8 constant_dynamic-update-slice_fusion.16
  512.5 2.9 constant_dynamic-update-slice_fusion.15
  519.0 2.2 constant_dynamic-update-slice_fusion.12
  521.3 15.0 %fusion.3 = f32[1280,2048]{1,0:T(8,128)S(1)} fusion(bf16[1280,2048]{1,0:T(8,128)(2,1)} %all-gather.6.cloned.1.call-done, bf16[4096,2048]{1,0:T(8,128)(2,1)} %constant_dynamic-update-slice_fusion.12, s32[]{:T(128)S(6)} %select_n.63), kind=kOutput, calls=%fused_computation.11 | convolution fusion | flops 10737418240 | bytes 24117252 | tf_op jit(solution)/shard_map/dot_general | solution.py:54
  537.9 2.2 copy-done.5
  541.8 9.6 convolution_convert_fusion.3
  551.4 86.2 %reduce-scatter.11.cloned.1.call-done = bf16[160,2048]{1,0:T(8,128)(2,1)} async-done(((bf16[1280,2048]{1,0:T(8,128)(2,1)}), bf16[160,2048]{1,0:T(8,128)(2,1)}) %reduce-scatter.11.cloned.1.call-update) | async-done | bytes 655376 | tf_op jit(solution)/shard_map/reduce_scatter | solution.py:98
  640.6 2.3 fusion.47
  643.2 54.5 %all-gather.8.cloned.1.call-done = bf16[1280,2048]{1,0:T(8,128)(2,1)} async-done(((bf16[160,2048]{1,0:T(8,128)(2,1)}), bf16[1280,2048]{1,0:T(8,128)(2,1)}) %all-gather.8.cloned.1.call-update) | async-done | bytes 5242896 | tf_op jit(solution)/shard_map/all_gather | solution.py:94
  697.7 13.0 %multiply_convert_fusion.1 = (bf16[1280,1024]{1,0:T(8,128)(2,1)S(1)}, bf16[1280,1024]{1,0:T(8,128)(2,1)S(1)}) fusion(f32[1280,2048]{1,0:T(8,128)} %copy-done.5, bf16[1280,2048]{1,0:T(8,128)(2,1)} %all-gather.8.cloned.1.call-done, bf16[4096,1024]{1,0:T(8,128)(2,1)} %copy-done.33, s32[]{:T(128)S(6)} %select_n.63), kind=kOutput, calls=%fused_computation.22 | convolution fusion | flops 5385748480 | bytes 25165828 | tf_op jit(solution)/shard_map/dot_general | solution.py:54
  713.1 15.3 %convolution_convert_fusion.2 = bf16[1280,2048]{1,0:T(8,128)(2,1)} fusion(bf16[4096,2048]{1,0:T(8,128)(2,1)} %constant_dynamic-update-slice_fusion.12, s32[]{:T(128)S(6)} %select_n.63, bf16[1280,1024]{1,0:T(8,128)(2,1)S(1)} %get-tuple-element.38, bf16[1280,1024]{1,0:T(8,128)(2,1)S(1)} %get-tuple-element.37), kind=kOutput, calls=%fused_computation.7 | convolution fusion | flops 10750525440 | bytes 18874372 | tf_op jit(solution)/shard_map/dot_general | solution.py:58
  728.5 58.6 %reduce-scatter.13.cloned.1.call-done = bf16[160,2048]{1,0:T(8,128)(2,1)} async-done(((bf16[1280,2048]{1,0:T(8,128)(2,1)}), bf16[160,2048]{1,0:T(8,128)(2,1)}) %reduce-scatter.13.cloned.1.call-update) | async-done | bytes 655376 | tf_op jit(solution)/shard_map/reduce_scatter | solution.py:98
  787.1 1.7 fusion.53
  788.8 3.1 fusion.52
  792.2 10.3 convolution_convert_fusion.5
  802.5 16.7 %convolution_convert_fusion = bf16[2048,2048]{1,0:T(8,128)(2,1)} fusion(bf16[1280,2048]{1,0:T(8,128)(2,1)} %all-gather.6.cloned.1.call-done, bf16[1280,1024]{1,0:T(8,128)(2,1)} %copy-done.42, bf16[1280,1024]{1,0:T(8,128)(2,1)} %copy-done.41), kind=kOutput, calls=%fused_computation.5 | convolution fusion | flops 10752098304 | bytes 18874368 | tf_op jit(solution)/shard_map/dot_general | solution.py:62
  819.6 27.1 %all-gather.10.cloned.1.call-done = bf16[1280,2048]{1,0:T(8,128)(2,1)} async-done(((bf16[160,2048]{1,0:T(8,128)(2,1)}), bf16[1280,2048]{1,0:T(8,128)(2,1)}) %all-gather.10.cloned.1.call-update) | async-done | bytes 5242896 | tf_op jit(solution)/shard_map/all_gather | solution.py:94
  846.7 4.7 multiply_reduce_fusion.2
  851.4 6.3 fusion.1
  857.8 2.2 convolution_bitcast_fusion
  862.8 1.8 copy-done.2
  865.4 22.7 %psum.15 = f32[2,1280]{1,0:T(2,128)S(1)} all-reduce(f32[2,1280]{1,0:T(2,128)S(1)} %pad_maximum_fusion.15), channel_id=1, replica_groups=mesh['dp'=4,'seq'=8] {'seq'}, use_global_device_ids=true, to_apply=%region_14.15 | all-reduce | flops 2560 | bytes 20480 | tf_op jit(solution)/shard_map/psum | solution.py:231
  888.1 5.4 convolution_convert_fusion.6
  894.0 2.6 multiply_convert_fusion.4
  896.7 7.5 fusion.35
  904.2 5.6 fusion.24
  909.8 2.4 fusion.16
  913.8 8.1 convolution_convert_fusion.1
  921.9 33.5 %all_to_all.126 = bf16[8,64,1024]{2,1,0:T(8,128)(2,1)} all-to-all(bf16[8,64,1024]{2,1,0:T(8,128)(2,1)} %bitcast.207), channel_id=1, replica_groups=mesh['dp'=4,'seq'=8] {'seq'}, dimensions={0} | all-to-all | bytes 2097152 | tf_op jit(solution)/shard_map/all_to_all | solution.py:106
  955.4 36.8 %reduce-scatter.21.cloned.1.call-done = bf16[512,2048]{1,0:T(8,128)(2,1)} async-done(((bf16[2048,2048]{1,0:T(8,128)(2,1)}), bf16[512,2048]{1,0:T(8,128)(2,1)}) %reduce-scatter.21.cloned.1.call-update) | async-done | bytes 2097168 | tf_op jit(solution)/shard_map/reduce_scatter | solution.py:104
  992.3 51.5 %all_to_all.127 = bf16[8,64,2048]{2,1,0:T(8,128)(2,1)S(1)} all-to-all(bf16[8,64,2048]{2,1,0:T(8,128)(2,1)} %bitcast.199), channel_id=1, replica_groups=mesh['dp'=4,'seq'=8] {'seq'}, dimensions={0} | all-to-all | bytes 4194304 | tf_op jit(solution)/shard_map/all_to_all | solution.py:106
  1043.8 6.3 all-to-all-start.5
  1050.1 24.9 %reduce-scatter.17.cloned.1.call-done = bf16[512,896]{0,1:T(8,128)(2,1)} async-done(((bf16[2048,896]{0,1:T(8,128)(2,1)}), bf16[512,896]{0,1:T(8,128)(2,1)}) %reduce-scatter.17.cloned.1.call-update) | async-done | bytes 917520 | tf_op jit(solution)/shard_map/reduce_scatter | solution.py:104
  1075.0 2.2 copy.129
  1077.2 5.5 all-to-all-start.4
  1089.9 26.8 %all-to-all-done.4 = bf16[8,64,896]{2,1,0:T(8,128)(2,1)} async-done(((bf16[8,64,896]{2,1,0:T(8,128)(2,1)}), bf16[8,64,896]{2,1,0:T(8,128)(2,1)}, u32[]{:S(2)}, u32[]{:S(2)}) %all-to-all-start.4) | async-done | bytes 917536 | tf_op jit(solution)/shard_map/all_to_all | solution.py:106
  1122.2 32.8 %reduce-scatter.15.cloned.1.call-done = bf16[160,2048]{1,0:T(8,128)(2,1)} async-done(((bf16[1280,2048]{1,0:T(8,128)(2,1)}), bf16[160,2048]{1,0:T(8,128)(2,1)}) %reduce-scatter.15.cloned.1.call-update) | async-done | bytes 655376 | tf_op jit(solution)/shard_map/reduce_scatter | solution.py:98
  1155.0 2.2 fusion.72
  (229 shorter events, 65.9 us)
Async XLA Ops:
  7.2 9.8 copy-start.26
  7.2 9.9 copy-start.27
  7.2 9.9 copy-start.28
  7.2 130.2 %all-gather.12.cloned.1.call-start = ((), (), s32[]{:S(2)}) async-start(), calls=%async_computation.27 | async-start | bytes 5898240 | tf_op jit(solution)/shard_map/all_gather | solution.py:94
  9.9 8.4 copy-start.40
  9.9 9.6 copy-start.38
  9.9 10.2 copy-start.39
  10.7 23.4 %all-to-all-start.1 = ((bf16[64,8,384]{2,0,1:T(8,128)(2,1)}), bf16[64,8,384]{2,0,1:T(8,128)(2,1)S(1)}, u32[]{:S(2)}, u32[]{:S(2)}) async-start(bf16[64,8,384]{2,0,1:T(8,128)(2,1)} %copy.115), calls=%async_computation.1 | async-start | bytes 786432 | tf_op jit(solution)/shard_map/all_to_all | solution.py:73
  34.1 44.9 %all-to-all-start = ((bf16[64,8,768]{2,0,1:T(8,128)(2,1)}), bf16[64,8,768]{2,0,1:T(8,128)(2,1)S(1)}, u32[]{:S(2)}, u32[]{:S(2)}) async-start(bf16[64,8,768]{2,0,1:T(8,128)(2,1)} %copy.113), calls=%async_computation | async-start | bytes 1572864 | tf_op jit(solution)/shard_map/all_to_all | solution.py:73
  40.9 263.2 %reduce-scatter.9.cloned.1.call-start = ((), (), s32[]{:S(2)}) async-start(), calls=%async_computation.16 | async-start | bytes 5898240 | tf_op jit(solution)/shard_map/reduce_scatter | solution.py:98
  43.7 37.4 %collective-permute-start.2 = (bf16[512,384]{1,0:T(8,128)(2,1)S(1)}, bf16[512,384]{1,0:T(8,128)(2,1)S(1)}, u32[]{:S(2)}, u32[]{:S(2)}) collective-permute-start(bf16[512,384]{1,0:T(8,128)(2,1)S(1)} %bitcast.185), channel_id=1, source_target_pairs={{0,24},{8,0},{16,8},{24,16},{1,25},{9,1},{17,9},{25,17},{2,26},{10... | collective-permute-start | bytes 1179656 | tf_op jit(solution)/shard_map/ppermute | solution.py:81
  79.0 18.7 %collective-permute-start = (bf16[512,768]{1,0:T(8,128)(2,1)S(1)}, bf16[512,768]{1,0:T(8,128)(2,1)S(1)}, u32[]{:S(2)}, u32[]{:S(2)}) collective-permute-start(bf16[512,768]{1,0:T(8,128)(2,1)S(1)} %bitcast.176), channel_id=1, source_target_pairs={{0,24},{8,0},{16,8},{24,16},{1,25},{9,1},{17,9},{25,17},{2,26},{10... | collective-permute-start | bytes 2359304 | tf_op jit(solution)/shard_map/ppermute | solution.py:81
  81.2 18.5 %collective-permute-start.3 = (bf16[1024,384]{1,0:T(8,128)(2,1)S(1)}, bf16[1024,384]{1,0:T(8,128)(2,1)S(1)}, u32[]{:S(2)}, u32[]{:S(2)}) collective-permute-start(bf16[1024,384]{1,0:T(8,128)(2,1)S(1)} %pad_maximum_fusion.11), channel_id=1, source_target_pairs={{0,16},{8,24},{16,0},{24,8},{1,17},{9,25},{17,1},{25,9},{2,18},{10... | collective-permute-start | bytes 2359304 | tf_op jit(solution)/shard_map/ppermute | solution.py:81
  97.8 35.2 %collective-permute-start.1 = (bf16[1024,768]{1,0:T(8,128)(2,1)S(1)}, bf16[1024,768]{1,0:T(8,128)(2,1)S(1)}, u32[]{:S(2)}, u32[]{:S(2)}) collective-permute-start(bf16[1024,768]{1,0:T(8,128)(2,1)S(1)} %pad_maximum_fusion.7), channel_id=1, source_target_pairs={{0,16},{8,24},{16,0},{24,8},{1,17},{9,25},{17,1},{25,9},{2,18},{10... | collective-permute-start | bytes 4718600 | tf_op jit(solution)/shard_map/ppermute | solution.py:81
  100.2 1.7 copy-start.19
  103.5 68.8 %copy-start.34 = (f32[256]{0:T(256)}, f32[256]{0:T(256)S(1)}, u32[]{:S(2)}) copy-start(f32[256]{0:T(256)S(1)} %get-tuple-element.79) | copy-start | bytes 3076
  103.5 68.8 %copy-start.36 = (f32[256]{0:T(256)}, f32[256]{0:T(256)S(1)}, u32[]{:S(2)}) copy-start(f32[256]{0:T(256)S(1)} %get-tuple-element.80) | copy-start | bytes 3076
  145.2 1.9 copy-start.1
  172.3 2.2 copy-start.29
  172.3 2.2 copy-start.31
  175.6 1.5 copy-start.18
  176.1 4.5 copy-start.13
  180.6 5.1 copy-start
  191.7 1.8 copy-start.21
  196.8 111.1 %all-to-all-start.2 = ((bf16[64,8,2048]{2,0,1:T(8,128)(2,1)}), bf16[64,8,2048]{2,0,1:T(8,128)(2,1)S(1)}, u32[]{:S(2)}, u32[]{:S(2)}) async-start(bf16[64,8,2048]{2,0,1:T(8,128)(2,1)} %copy.119), calls=%async_computation.3 | async-start | bytes 4194304 | tf_op jit(solution)/shard_map/all_to_all | solution.py:73
  206.4 314.8 %all-gather.6.cloned.1.call-start = ((), (), s32[]{:S(2)}) async-start(), calls=%async_computation.17 | async-start | bytes 5898240 | tf_op jit(solution)/shard_map/all_gather | solution.py:94
  307.8 329.9 %reduce-scatter.11.cloned.1.call-start = ((), (), s32[]{:S(2)}) async-start(), calls=%async_computation.18 | async-start | bytes 5898240 | tf_op jit(solution)/shard_map/reduce_scatter | solution.py:98
  307.9 67.3 %collective-permute-start.4 = (bf16[512,2048]{1,0:T(8,128)(2,1)S(1)}, bf16[512,2048]{1,0:T(8,128)(2,1)S(1)}, u32[]{:S(2)}, u32[]{:S(2)}) collective-permute-start(bf16[512,2048]{1,0:T(8,128)(2,1)S(1)} %bitcast.168), channel_id=1, source_target_pairs={{0,24},{8,0},{16,8},{24,16},{1,25},{9,1},{17,9},{25,17},{2,26},{10... | collective-permute-start | bytes 6291464 | tf_op jit(solution)/shard_map/ppermute | solution.py:81
  374.8 22.4 %collective-permute-start.6 = (bf16[512,1024]{1,0:T(8,128)(2,1)S(1)}, bf16[512,1024]{1,0:T(8,128)(2,1)S(1)}, u32[]{:S(2)}, u32[]{:S(2)}) collective-permute-start(bf16[512,1024]{1,0:T(8,128)(2,1)S(1)} %bitcast.172), channel_id=1, source_target_pairs={{0,24},{8,0},{16,8},{24,16},{1,25},{9,1},{17,9},{25,17},{2,26},{10... | collective-permute-start | bytes 3145736 | tf_op jit(solution)/shard_map/ppermute | solution.py:81
  375.7 136.8 %collective-permute-start.5 = (bf16[1024,2048]{1,0:T(8,128)(2,1)S(1)}, bf16[1024,2048]{1,0:T(8,128)(2,1)S(1)}, u32[]{:S(2)}, u32[]{:S(2)}) collective-permute-start(bf16[1024,2048]{1,0:T(8,128)(2,1)S(1)} %pad_maximum_fusion.1), channel_id=1, source_target_pairs={{0,16},{8,24},{16,0},{24,8},{1,17},{9,25},{17,1},{25,9},{2,18},{10... | collective-permute-start | bytes 12582920 | tf_op jit(solution)/shard_map/ppermute | solution.py:81
  397.4 112.8 %collective-permute-start.7 = (bf16[1024,1024]{1,0:T(8,128)(2,1)S(1)}, bf16[1024,1024]{1,0:T(8,128)(2,1)S(1)}, u32[]{:S(2)}, u32[]{:S(2)}) collective-permute-start(bf16[1024,1024]{1,0:T(8,128)(2,1)S(1)} %pad_maximum_fusion.5), channel_id=1, source_target_pairs={{0,16},{8,24},{16,0},{24,8},{1,17},{9,25},{17,1},{25,9},{2,18},{10... | collective-permute-start | bytes 6291464 | tf_op jit(solution)/shard_map/ppermute | solution.py:81
  510.7 5.2 copy-start.33
  536.3 3.9 copy-start.5
  540.1 1.6 copy-start.15
  551.4 87.6 %copy-start.3 = (bf16[1,160,2048]{2,1,0:T(8,128)(2,1)S(1)}, bf16[1,160,2048]{2,1,0:T(8,128)(2,1)}, u32[]{:S(2)}) copy-start(bf16[1,160,2048]{2,1,0:T(8,128)(2,1)} %param.28) | copy-start | bytes 1966084
  551.4 146.3 %all-gather.8.cloned.1.call-start = ((), (), s32[]{:S(2)}) async-start(), calls=%async_computation.19 | async-start | bytes 5898240 | tf_op jit(solution)/shard_map/all_gather | solution.py:94
  643.0 144.1 %reduce-scatter.13.cloned.1.call-start = ((), (), s32[]{:S(2)}) async-start(), calls=%async_computation.20 | async-start | bytes 5898240 | tf_op jit(solution)/shard_map/reduce_scatter | solution.py:98
  710.8 1.5 copy-start.41
  710.8 2.3 copy-start.42
  728.4 58.7 %copy-start.4 = (bf16[160,2048]{1,0:T(8,128)(2,1)S(1)}, bf16[160,2048]{1,0:T(8,128)(2,1)}, u32[]{:S(2)}) copy-start(bf16[160,2048]{1,0:T(8,128)(2,1)} %reduce-scatter.9.cloned.1.call-done) | copy-start | bytes 1966084
  728.4 60.4 %copy-start.6 = (bf16[160,2048]{1,0:T(8,128)(2,1)S(1)}, bf16[160,2048]{1,0:T(8,128)(2,1)}, u32[]{:S(2)}) copy-start(bf16[160,2048]{1,0:T(8,128)(2,1)} %reduce-scatter.11.cloned.1.call-done) | copy-start | bytes 1966084
  728.4 118.3 %all-gather.10.cloned.1.call-start = ((), (), s32[]{:S(2)}) async-start(), calls=%async_computation.21 | async-start | bytes 5898240 | tf_op jit(solution)/shard_map/all_gather | solution.py:94
  791.9 130.0 %reduce-scatter.23.cloned.1.call-start = ((), (), s32[]{:S(2)}) async-start(), calls=%async_computation.26 | async-start | bytes 5242880 | tf_op jit(solution)/shard_map/reduce_scatter | solution.py:104
  802.5 189.8 %reduce-scatter.21.cloned.1.call-start = ((), (), s32[]{:S(2)}) async-start(), calls=%async_computation.25 | async-start | bytes 10485760 | tf_op jit(solution)/shard_map/reduce_scatter | solution.py:104
  819.2 224.5 %reduce-scatter.19.cloned.1.call-start = ((), (), s32[]{:S(2)}) async-start(), calls=%async_computation.24 | async-start | bytes 1310720 | tf_op jit(solution)/shard_map/reduce_scatter | solution.py:104
  851.4 6.4 copy-start.9
  851.4 6.3 copy-start.14
  857.8 2.2 copy-start.7
  862.4 2.2 copy-start.2
  862.4 2.2 copy-start.30
  862.4 2.2 copy-start.32
  862.4 2.2 copy-start.35
  862.4 2.2 copy-start.37
  893.6 181.4 %reduce-scatter.17.cloned.1.call-start = ((), (), s32[]{:S(2)}) async-start(), calls=%async_computation.23 | async-start | bytes 4587520 | tf_op jit(solution)/shard_map/reduce_scatter | solution.py:104
  894.0 2.7 copy-start.10
  894.0 10.2 slice-start
  896.6 7.6 copy-start.22
  896.6 7.6 copy-start.24
  896.7 7.5 slice-start.1
  912.2 1.6 copy-start.25
  912.2 242.8 %reduce-scatter.15.cloned.1.call-start = ((), (), s32[]{:S(2)}) async-start(), calls=%async_computation.22 | async-start | bytes 5898240 | tf_op jit(solution)/shard_map/reduce_scatter | solution.py:98
  1043.8 33.4 %all-to-all-start.5 = ((bf16[8,64,256]{2,1,0:T(8,128)(2,1)}), bf16[8,64,256]{2,1,0:T(8,128)(2,1)S(1)}, u32[]{:S(2)}, u32[]{:S(2)}) async-start(bf16[8,64,256]{2,1,0:T(8,128)(2,1)} %bitcast.224), calls=%async_computation.11 | async-start | bytes 524288 | tf_op jit(solution)/shard_map/all_to_all | solution.py:106
  1077.2 39.4 %all-to-all-start.4 = ((bf16[8,64,896]{2,1,0:T(8,128)(2,1)}), bf16[8,64,896]{2,1,0:T(8,128)(2,1)}, u32[]{:S(2)}, u32[]{:S(2)}) async-start(bf16[8,64,896]{2,1,0:T(8,128)(2,1)} %bitcast.198), calls=%async_computation.9 | async-start | bytes 1835008 | tf_op jit(solution)/shard_map/all_to_all | solution.py:106
  1089.9 65.1 %copy-start.8 = (bf16[160,2048]{1,0:T(8,128)(2,1)S(1)}, bf16[160,2048]{1,0:T(8,128)(2,1)}, u32[]{:S(2)}) copy-start(bf16[160,2048]{1,0:T(8,128)(2,1)} %reduce-scatter.13.cloned.1.call-done) | copy-start | bytes 1966084
  (6 other events, 6.8 us)
Sparse Core Ops, SparseCore 0:
  9.7 75.1 all-gather.11
  191.8 112.1 reduce-scatter.8
  307.9 82.6 all-gather.5
  551.5 86.0 reduce-scatter.10
  643.1 54.5 all-gather.7
  728.5 58.4 reduce-scatter.12
  792.1 54.5 all-gather.9
  849.6 52.8 reduce-scatter.22
  905.9 86.3 reduce-scatter.20
  995.6 27.7 reduce-scatter.18
  1026.6 48.3 reduce-scatter.16
  1077.3 77.6 reduce-scatter.14
